TPU v7x, 32 devices: a whole 2x2x4 slice. The times are simulated.
32 devices in a mesh: ctx: 8 (over y, x, core), exp: 4 (over z).
Axes of the slice: x: 2, y: 2, z: 4, core: 2. Of those that a mesh axis runs over, the one named last changes fastest.
Arguments:
- mixer_input: bfloat16 [8192, 4096], P('ctx', 'exp'), may hold values from -6 to 6
- scale_exponent: int32 [64, 64], P('ctx', 'exp'), may hold values from -1 to 1
- step_size: float32 [64, 8192], P('exp', 'ctx'), may hold values from 0.25 to 1
- decay_log: float32 [64, 8192], P('exp', 'ctx'), may hold values from -1.2 to 0
- state_input: bfloat16 [8192, 128], P('ctx'), may hold values from -6 to 6
- state_output: bfloat16 [8192, 128], P('ctx'), may hold values from -0.5 to 0.5
- skip_gain: float32 [64], P('exp'), may hold values from 0.5 to 1.5
- gate_input: bfloat16 [8192, 4096], P('ctx', 'exp'), may hold values from -6 to 6
- norm_gain: float32 [4096], P('exp'), may hold values from 0.25 to 1.75
- up_weight: bfloat16 [4096, 3072], P('ctx', 'exp'), may hold values from -0.09375 to 0.09375
- down_weight: bfloat16 [3072, 4096], P('exp', 'ctx'), may hold values from -0.15625 to 0.15625
- expert_slot: int32 [8192], P('ctx'), may hold values from 0 to 256, as said below
- gate_prob: float32 [8192], P('ctx'), may hold values from 0.2 to 1
Outputs:
- layer_out: bfloat16 [8192, 4096], P('ctx', 'exp')
Inputs may be any that keep to these rules, and one draw needn't show every extreme that they name: `expert_slot`: within each aligned block of 1024 tokens, the tokens routed to the expert carry the distinct slots 0 to k - 1 for some k of at most 256, and all other tokens carry 256; in some block k equals 256.
All inputs are finite; a program needn't handle non-finite values.
Results may differ from a plain program's by a relative error of at most 0.0085.
Values may be sent and summed in bfloat16 or wider, within the bound.
No kernel may reach another device: no remote copies, remote signals or barrier semaphores. Data moves between devices by JAX's collectives and lax.ppermute only.
A program may use at most 128 MiB of HBM per device.

v0:
```python
import jax
import jax.numpy as jnp
from jax import lax
from jax.sharding import PartitionSpec as P

P_SIZE = 64
BLK = 128
CAP = 256
highest = lax.Precision.HIGHEST


def local_scan(x_in, step_size, decay_log, b_rows, c_rows):
    length, head_count, head_width = x_in.shape
    blocks = length // BLK
    x_blocks = x_in.reshape(blocks, BLK, head_count, head_width)
    b_blocks = b_rows.reshape(blocks, BLK, b_rows.shape[1])
    c_blocks = c_rows.reshape(blocks, BLK, c_rows.shape[1])
    step_blocks = step_size.reshape(head_count, blocks, BLK)
    cumulative = jnp.cumsum(decay_log.reshape(head_count, blocks, BLK), axis=2)
    scores = jnp.einsum("bin,bjn->bij", c_blocks, b_blocks, precision=highest)
    causal = jnp.arange(BLK)[:, None] >= jnp.arange(BLK)[None, :]
    spread = jnp.where(causal, cumulative[:, :, :, None] - cumulative[:, :, None, :], -jnp.inf)
    mixing = jnp.exp(spread) * scores[None] * step_blocks[:, :, None, :]
    inner_part = jnp.einsum("hbij,bjhp->bihp", mixing, x_blocks, precision=highest)
    tail_decay = jnp.exp(cumulative[:, :, -1:] - cumulative) * step_blocks
    block_state = jnp.einsum(
        "hbj,bjn,bjhp->bhnp", tail_decay, b_blocks, x_blocks, precision=highest
    )
    totals = cumulative[:, :, -1]

    def carry_on(running, block_items):
        block_total, block_end = block_items
        return (jnp.exp(block_total)[:, None, None] * running + block_end, running)

    running, entering = lax.scan(
        carry_on, jnp.zeros(block_state.shape[1:], jnp.float32), (totals.T, block_state)
    )
    carried = jnp.einsum(
        "bin,hbi,bhnp->bihp", c_blocks, jnp.exp(cumulative), entering, precision=highest
    )
    offsets = jnp.cumsum(totals, axis=1) - totals
    growth = jnp.exp(offsets[:, :, None] + cumulative)
    return (inner_part + carried, running, jnp.sum(totals, axis=1), c_blocks, growth)


def body(
    mixer_input,
    scale_exponent,
    step_size,
    decay_log,
    state_input,
    state_output,
    skip_gain,
    gate_input,
    norm_gain,
    up_weight,
    down_weight,
    expert_slot,
    gate_prob,
):
    length = mixer_input.shape[0]
    head_count = skip_gain.shape[0]
    blocks = length // BLK
    factor = jnp.exp2(scale_exponent.astype(jnp.float32))
    x_in = (
        mixer_input.astype(jnp.float32).reshape(blocks, BLK, head_count, P_SIZE)
        * factor[:, None, :, None]
    ).reshape(length, head_count, P_SIZE)
    b_rows = state_input.astype(jnp.float32)
    c_rows = state_output.astype(jnp.float32)
    local_out, end_state, total_log, c_blocks, growth = local_scan(
        x_in, step_size, decay_log, b_rows, c_rows
    )
    log_totals = lax.all_gather(total_log[None, :], "ctx", axis=0, tiled=True)
    before = jnp.cumsum(log_totals, axis=0) - log_totals
    position = lax.axis_index("ctx")
    own_prior = lax.dynamic_index_in_dim(before, position, 0, keepdims=False)
    shard_piece = lax.all_gather(
        end_state[None].astype(jnp.bfloat16), "ctx", axis=0, tiled=True
    ).astype(jnp.float32)
    row_count = shard_piece.shape[0]
    row_ids = jnp.arange(row_count, dtype=jnp.int32)
    decay_gap = jnp.minimum(own_prior[None, :] - before - log_totals, 0.0)
    weight = jnp.where((row_ids < position)[:, None], jnp.exp(decay_gap), 0.0)
    start_state = jnp.zeros_like(end_state) + jnp.einsum(
        "kh,khnp->hnp", weight, shard_piece, precision=highest
    )
    handed = jnp.einsum("bin,hbi,hnp->bihp", c_blocks, growth, start_state, precision=highest)
    mixer_out = (local_out + handed).reshape(length, head_count, P_SIZE) + skip_gain[
        None, :, None
    ] * x_in
    gated_out = mixer_out * jax.nn.silu(
        gate_input.astype(jnp.float32).reshape(length, head_count, P_SIZE)
    )
    inverse_rms = lax.rsqrt(jnp.mean(gated_out * gated_out, axis=2, keepdims=True) + 1e-05)
    normed = (
        (gated_out * inverse_rms * norm_gain.reshape(head_count, P_SIZE))
        .reshape(length, head_count * P_SIZE)
        .astype(jnp.bfloat16)
    )
    places = jnp.arange(CAP, dtype=jnp.int32)[:, None] == expert_slot[None, :]
    picker = places.astype(jnp.bfloat16)
    dispatched = jnp.dot(picker, normed, preferred_element_type=jnp.float32).astype(jnp.bfloat16)
    full_features = lax.all_gather(dispatched, "exp", axis=1, tiled=True)
    up_act = jnp.dot(
        full_features,
        lax.all_gather(up_weight, "ctx", axis=0, tiled=True),
        preferred_element_type=jnp.float32,
    )
    hidden = jax.nn.silu(up_act).astype(jnp.bfloat16)
    terms = jnp.dot(
        hidden,
        lax.all_gather(down_weight, "ctx", axis=1, tiled=True),
        preferred_element_type=jnp.float32,
    )
    own_sums = lax.psum_scatter(
        terms.astype(jnp.bfloat16), "exp", scatter_dimension=1, tiled=True
    ).astype(jnp.float32)
    selector = places.astype(jnp.float32)
    expert_tok = lax.dot_general(selector, own_sums, (((0,), (0,)), ((), ())), precision=highest)
    return (normed.astype(jnp.float32) + gate_prob[:, None] * expert_tok).astype(jnp.bfloat16)


def solution(mesh):
    in_specs = (
        P("ctx", "exp"),
        P("ctx", "exp"),
        P("exp", "ctx"),
        P("exp", "ctx"),
        P("ctx", None),
        P("ctx", None),
        P("exp"),
        P("ctx", "exp"),
        P("exp"),
        P("ctx", "exp"),
        P("exp", "ctx"),
        P("ctx"),
        P("ctx"),
    )
    out_specs = P("ctx", "exp")
    return jax.shard_map(body, mesh=mesh, in_specs=in_specs, out_specs=out_specs, check_vma=False)
```

profile of v0, /device:TPU:0, one launch (start us, length us, event | category | flops | bytes accessed | tf_op | source)
XLA Modules:
  0.0 375.8 jit_solution(6003521538814983370)
XLA Ops:
  6.5 0.9 copy.117
  7.4 4.5 %reduce_window_sum.33 = f32[16,8,128]{2,1,0:T(8,128)S(1)} reduce-window(f32[16,8,128]{2,1,0:T(8,128)S(1)} %bitcast.107, f32[]{:T(128)} %constant.28.clone.1), window={size=1x1x128 pad=0_0x0_0x127_0}, to_apply=%region_0.0 | reduce-window | flops 2080768 | bytes 131076 | tf_op jit(solution)/shard_map/jit(cumsum)/reduce_window_sum | solution.py:19
  12.4 0.3 slice_reduce_fusion
  12.9 0.9 copy.118
  13.9 0.7 multiply_exponential_fusion
  14.6 6.8 %reshape.91 = f32[8,128,16,64]{3,2,1,0:T(8,128)} reshape(bf16[1024,1024]{1,0:T(8,128)(2,1)} %param.15) | data formatting | bytes 6291456 | tf_op jit(solution)/shard_map/reshape | solution.py:66
  21.4 7.2 %copy.74 = f32[8,128,16,64]{1,3,2,0:T(8,128)} copy(f32[8,128,16,64]{3,2,1,0:T(8,128)} %reshape.91) | data formatting | bytes 8388608 | tf_op jit(solution)/shard_map/reshape | solution.py:66
  28.5 6.4 %fusion.20 = f32[8,16,128,64]{2,3,1,0:T(8,128)} fusion(bf16[8,128,128,1]{2,1,3,0:T(8,128)(2,1)S(1)} %bitcast.102, f32[8,128,16,64]{1,3,2,0:T(8,128)} %copy.74, f32[8,128,16]{1,2,0:T(8,128)S(1)} %copy.81, f32[8,16]{1,0:T(8,128)S(1)} %multiply_exponential_fusion), kind=kOutput, calls=%fused_computation.31 | convolution fusion | flops 1612709888 | bytes 8716800 | tf_op jit(solution)/shard_map/hbj,bjn,bjhp->bhnp/dot_general | solution.py:26
  35.0 21.8 %while.13 = (s32[]{:T(128)}, f32[16,128,64]{2,1,0:T(8,128)S(1)}, f32[8,16,128,64]{3,2,1,0:T(8,128)}, f32[8,16]{1,0:T(8,128)S(1)}, f32[8,16,128,64]{2,3,1,0:T(8,128)}, /*index=5*/s32[]{:T(128)}, s32[]{:T(128)}) while((s32[]{:T(128)}, f32[16,128,64]{2,1,0:T(8,128)S(1)}, f32[8,16,128,64]{3,2,1,0:T(8,128)}, f32[8,16]{1,0:T(8,128)S(1)}, ...), condition=%wide.region_2.3_spmd.clone, body=%wide.region_1.2_spmd.clone.sunk | while | flops 524291 | bytes 5243680 | solution.py:35
  35.0 1.0 bitcast_dynamic-update-slice_fusion.2
  36.0 1.1 constant_dynamic-slice_fusion.3
  37.1 0.3 copy.125
  37.4 0.2 bitcast_add_fusion.2
  37.7 1.1 bitcast_dynamic-update-slice_fusion.2
  38.8 1.1 constant_dynamic-slice_fusion.3
  39.8 0.3 copy.125
  40.2 0.2 bitcast_add_fusion.2
  40.4 1.1 bitcast_dynamic-update-slice_fusion.2
  41.5 1.1 constant_dynamic-slice_fusion.3
  42.6 0.3 copy.125
  43.1 1.1 bitcast_dynamic-update-slice_fusion.2
  44.2 1.1 constant_dynamic-slice_fusion.3
  45.3 0.3 copy.125
  45.8 1.0 bitcast_dynamic-update-slice_fusion.2
  46.9 1.1 constant_dynamic-slice_fusion.3
  48.0 0.3 copy.125
  48.3 0.2 bitcast_add_fusion.2
  48.5 1.1 bitcast_dynamic-update-slice_fusion.2
  49.6 1.1 constant_dynamic-slice_fusion.3
  50.7 0.3 copy.125
  51.3 1.1 bitcast_dynamic-update-slice_fusion.2
  52.4 1.1 constant_dynamic-slice_fusion.3
  53.4 0.3 copy.125
  54.0 1.1 bitcast_dynamic-update-slice_fusion.2
  55.1 1.1 constant_dynamic-slice_fusion.3
  56.2 0.3 copy.125
  56.8 0.9 copy.87
  57.8 0.6 dynamic-slice
  59.1 0.2 dynamic-update-slice
  59.4 15.6 %all-reduce = f32[128]{0:T(128)S(1)} all-reduce(f32[128]{0:T(128)S(1)} %dynamic-update-slice), channel_id=2, replica_groups=mesh['ctx'=8,'exp'=4] {'ctx'}, use_global_device_ids=true, to_apply=%add | all-reduce | flops 128 | bytes 1024
  75.1 6.8 %reshape.93 = f32[8,128,16,64]{3,2,1,0:T(8,128)} reshape(bf16[1024,1024]{1,0:T(8,128)(2,1)} %param.22) | data formatting | bytes 6291456 | tf_op jit(solution)/shard_map/reshape | solution.py:93
  81.9 7.2 %copy.94 = f32[8,128,16,64]{1,3,2,0:T(8,128)} copy(f32[8,128,16,64]{3,2,1,0:T(8,128)} %reshape.93) | data formatting | bytes 8388608 | tf_op jit(solution)/shard_map/reshape | solution.py:93
  89.2 2.5 mul.135
  91.6 5.4 %copy.90 = f32[1024,1024]{1,0:T(8,128)} copy(f32[1024,1024]{0,1:T(8,128)} %bitcast.99) | data formatting | bytes 8388608 | tf_op jit(solution)/shard_map/mul | solution.py:66
  97.3 0.3 fusion.34
  97.6 12.1 %fusion.35 = f32[8,16,64,128]{3,2,1,0:T(8,128)} fusion(f32[8,16,128,64]{3,2,1,0:T(8,128)} %get-tuple-element.33, bf16[8,128,128,1]{2,1,3,0:T(8,128)(2,1)S(1)} %bitcast.96), kind=kOutput, calls=%fused_computation.60 | convolution fusion | flops 1610612736 | bytes 8650752 | tf_op jit(solution)/shard_map/bin,hbi,bhnp->bihp/dot_general | solution.py:38
  109.8 18.0 %fusion.2 = f32[8,16,64,128]{3,2,1,0:T(8,128)} fusion(f32[16,8,128]{2,0,1:T(8,128)S(1)} %copy_bitcast_fusion.2, f32[8,128,128]{2,1,0:T(8,128)S(1)} %fusion.34, f32[16,8,128]{2,0,1:T(8,128)S(1)} %copy.75, pred[128,128]{1,0:T(8,128)(4,1)S(1)} %iota_compare_fusion.3, f32[8,128,16,64]{1,3,2,0:T(8,128)S(1)} %copy-done.2, f32[8,16]{1,0:T(8,128)S(1)} %multiply_exponential_fusion), kind=kOutput, calls=%fused_computation.6 | convolution fusion | flops 1620049920 | bytes 9060864 | tf_op jit(solution)/shard_map/hbij,bjhp->bihp/dot_general | solution.py:24
  127.7 2.1 multiply_reduce_fusion
  129.8 9.3 %multiply_reduce_fusion.1 = (f32[8,128,16]{1,2,0:T(8,128)S(1)}, f32[8,128,16,64]{1,3,2,0:T(8,128)}) fusion(f32[8,128,16,64]{1,3,2,0:T(8,128)} %copy.94, f32[8,128,16,64]{1,3,2,0:T(8,128)} %copy.74, f32[16]{0:T(128)S(1)} %copy-done.9, f32[8,16]{1,0:T(8,128)S(1)} %multiply_exponential_fusion, bf16[8,128,128,1]{2,1,3,0:T(8,128)(2,1)S(1)} %bitcast.97, ...), kind=kOutput, calls=%fused_computation.20 | convolution fusion | flops 1625276416 | bytes 21955136 | tf_op jit(solution)/shard_map/bin,hbi,hnp->bihp/dot_general | solution.py:88
  139.1 7.1 %copy.110 = f32[8,128,16,64]{3,2,1,0:T(8,128)} copy(f32[8,128,16,64]{1,3,2,0:T(8,128)} %get-tuple-element.89) | data formatting | bytes 8388608 | tf_op jit(solution)/shard_map/reshape | solution.py:89
  146.3 7.6 %reshape.92 = f32[1024,1024]{1,0:T(8,128)} reshape(f32[8,128,16,64]{3,2,1,0:T(8,128)} %copy.110) | data formatting | bytes 8388608 | tf_op jit(solution)/shard_map/reshape | solution.py:89
  153.9 2.5 mul.146
  156.4 5.5 %copy.96 = f32[1024,1024]{1,0:T(8,128)} copy(f32[1024,1024]{0,1:T(8,128)} %bitcast.100) | data formatting | bytes 8388608 | tf_op jit(solution)/shard_map/mul | solution.py:97
  161.9 6.6 %multiply_convert_fusion = bf16[1024,1024]{1,0:T(8,128)(2,1)S(1)} fusion(f32[1024,1024]{1,0:T(8,128)} %copy.96, f32[1024,1024]{1,0:T(8,128)} %reshape.92, f32[1024,1024]{1,0:T(8,128)} %copy.90, f32[1024]{0:T(1024)S(1)} %copy-done.8, f32[1024]{0:T(1024)S(1)} %mul.131, bf16[1024,1024]{1,0:T(8,128)(2,1)S(1)} %copy-done.3, bf16[1024,1024]{1,0:T(8,128)(2,1)} %param.15), kind=kLoop, calls=%fused_computation.19 | loop fusion | flops 13631488 | bytes 18882560 | tf_op jit(solution)/shard_map/convert_element_type | solution.py:99
  168.5 1.3 copy-done.4
  169.9 1.5 convolution_convert_fusion.1
  171.5 0.7 all-gather.11.cloned.1.call-update
  172.2 0.5 all-gather.9.cloned.1.call-update
  172.8 43.8 %all-gather.7.cloned.1.call-done = bf16[256,4096]{1,0:T(8,128)(2,1)} async-done(((bf16[256,1024]{1,0:T(8,128)(2,1)}), bf16[256,4096]{1,0:T(8,128)(2,1)}) %all-gather.7.cloned.1.call-update) | async-done | bytes 2097168 | tf_op jit(solution)/shard_map/all_gather | solution.py:104
  216.6 47.3 %all-gather.11.cloned.1.call-done = bf16[768,4096]{1,0:T(8,128)(2,1)} async-done(((bf16[768,512]{1,0:T(8,128)(2,1)}), bf16[768,4096]{1,0:T(8,128)(2,1)}) %all-gather.11.cloned.1.call-update) | async-done | bytes 6291472 | tf_op jit(solution)/shard_map/all_gather | solution.py:113
  263.9 47.2 %all-gather.9.cloned.1.call-done = bf16[4096,768]{1,0:T(8,128)(2,1)} async-done(((bf16[512,768]{1,0:T(8,128)(2,1)}), bf16[4096,768]{1,0:T(8,128)(2,1)}) %all-gather.9.cloned.1.call-update) | async-done | bytes 6291472 | tf_op jit(solution)/shard_map/all_gather | solution.py:107
  311.1 11.1 %convolution_convert_fusion = bf16[256,4096]{1,0:T(8,128)(2,1)} fusion(bf16[768,4096]{1,0:T(8,128)(2,1)} %all-gather.11.cloned.1.call-done, bf16[256,4096]{1,0:T(8,128)(2,1)} %all-gather.7.cloned.1.call-done, bf16[4096,768]{1,0:T(8,128)(2,1)} %all-gather.9.cloned.1.call-done), kind=kOutput, calls=%fused_computation.12 | convolution fusion | flops 3223257088 | bytes 16777216 | tf_op jit(solution)/shard_map/dot_general | solution.py:111
  322.2 43.8 %reduce-scatter.2.cloned.1.call-done = bf16[256,1024]{1,0:T(8,128)(2,1)} async-done(((bf16[256,4096]{1,0:T(8,128)(2,1)}), bf16[256,1024]{1,0:T(8,128)(2,1)}) %reduce-scatter.2.cloned.1.call-update) | async-done | bytes 524304 | tf_op jit(solution)/shard_map/reduce_scatter | solution.py:116
  366.0 3.3 add_convert_fusion
  (74 shorter events, 2.6 us)
Async XLA Ops:
  6.5 90.8 %copy-start = (bf16[1024,128]{1,0:T(8,128)(2,1)S(1)}, bf16[1024,128]{1,0:T(8,128)(2,1)}, u32[]{:S(2)}) copy-start(bf16[1024,128]{1,0:T(8,128)(2,1)} %param.20) | copy-start | bytes 786436
  6.5 121.2 %all-gather.13.cloned.1.call-start = ((), (), s32[]{:S(2)}) async-start(), calls=%async_computation.5 | async-start | bytes 2359296 | tf_op jit(solution)/shard_map/all_gather | solution.py:78
  21.4 7.2 %copy-start.6 = (bf16[1024,128]{1,0:T(8,128)(2,1)S(1)}, bf16[1024,128]{1,0:T(8,128)(2,1)}, u32[]{:S(2)}) copy-start(bf16[1024,128]{1,0:T(8,128)(2,1)} %param.19) | copy-start | bytes 786436
  35.0 22.9 %copy-start.12 = (u32[32]{0:T(128)S(1)}, u32[32]{0:T(128)}, u32[]{:S(2)}) copy-start(u32[32]{0:T(128)} %constant.54) | copy-start | bytes 388
  57.7 158.9 %all-gather.7.cloned.1.call-start = ((), (), s32[]{:S(2)}) async-start(), calls=%async_computation.1 | async-start | bytes 2621440 | tf_op jit(solution)/shard_map/all_gather | solution.py:104
  91.6 5.4 %copy-start.9 = (f32[16]{0:T(128)S(1)}, f32[16]{0:T(128)}, u32[]{:S(2)}) copy-start(f32[16]{0:T(128)} %param.21) | copy-start | bytes 196
  91.6 5.7 %copy-start.7 = (f32[16,1024]{1,0:T(8,128)S(1)}, f32[16,1024]{1,0:T(8,128)}, u32[]{:S(2)}) copy-start(f32[16,1024]{1,0:T(8,128)} %param.17) | copy-start | bytes 196612
  97.6 12.1 %copy-start.2 = (f32[8,128,16,64]{1,3,2,0:T(8,128)S(1)}, f32[8,128,16,64]{1,3,2,0:T(8,128)}, u32[]{:S(2)}) copy-start(f32[8,128,16,64]{1,3,2,0:T(8,128)} %copy.74) | copy-start | bytes 12582916
  156.4 5.5 %copy-start.3 = (bf16[1024,1024]{1,0:T(8,128)(2,1)S(1)}, bf16[1024,1024]{1,0:T(8,128)(2,1)}, u32[]{:S(2)}) copy-start(bf16[1024,1024]{1,0:T(8,128)(2,1)} %param.22) | copy-start | bytes 6291460
  156.4 5.5 %copy-start.8 = (f32[1024]{0:T(1024)S(1)}, f32[1024]{0:T(1024)}, u32[]{:S(2)}) copy-start(f32[1024]{0:T(1024)} %param.23) | copy-start | bytes 12292
  161.9 7.9 %copy-start.10 = (s32[1024]{0:T(1024)S(1)}, s32[1024]{0:T(1024)}, u32[]{:S(2)}) copy-start(s32[1024]{0:T(1024)} %param.26) | copy-start | bytes 12292
  168.5 1.3 copy-start.4
  171.4 92.5 %all-gather.11.cloned.1.call-start = ((), (), s32[]{:S(2)}) async-start(), calls=%async_computation.3 | async-start | bytes 7077888 | tf_op jit(solution)/shard_map/all_gather | solution.py:113
  172.2 138.9 %all-gather.9.cloned.1.call-start = ((), (), s32[]{:S(2)}) async-start(), calls=%async_computation.2 | async-start | bytes 7077888 | tf_op jit(solution)/shard_map/all_gather | solution.py:107
  172.7 193.2 %copy-start.5 = (bf16[1024,1024]{1,0:T(8,128)(2,1)S(1)}, bf16[1024,1024]{1,0:T(8,128)(2,1)}, u32[]{:S(2)}) copy-start(bf16[1024,1024]{1,0:T(8,128)(2,1)} %copy-done.4) | copy-start | bytes 6291460
  172.8 193.2 %copy-start.11 = (f32[1024]{0:T(1024)S(1)}, f32[1024]{0:T(1024)}, u32[]{:S(2)}) copy-start(f32[1024]{0:T(1024)} %param.27) | copy-start | bytes 12292
  172.8 193.2 %reduce-scatter.2.cloned.1.call-start = ((), (), s32[]{:S(2)}) async-start(), calls=%async_computation.4 | async-start | bytes 2621440 | tf_op jit(solution)/shard_map/reduce_scatter | solution.py:116
  311.1 58.2 %copy-start.1 = (bf16[1024,128]{1,0:T(8,128)(2,1)S(1)}, bf16[1024,128]{1,0:T(8,128)(2,1)}, u32[]{:S(2)}) copy-start(bf16[1024,128]{1,0:T(8,128)(2,1)} %param.20) | copy-start | bytes 786436
Sparse Core Ops, SparseCore 0:
  57.8 30.5 all-gather.12
  171.5 45.0 all-gather.6
  218.5 45.3 all-gather.10
  265.6 45.3 all-gather.8
  322.3 43.6 reduce-scatter.1
where the time goes:
time: 377 us; the launch traced here: 376 us
  waiting for transfers between devices  183 us (49%)
  local copies, waits for them, and re-layouts  75.8 us (20%)
  matrix products  62 us (16%)
  other arithmetic  24.6 us (7%)
  blocking collectives  15.6 us (4%)
  between operations  14 us (4%)
    all_gather x1, waiting for transfers between devices, body(): lax.all_gather(down_weight, 'ctx', axis=1, tiled=True)  47.3 us
    all_gather x1, waiting for transfers between devices, body(): lax.all_gather(up_weight, 'ctx', axis=0, tiled=True)  47.2 us
    all_gather x1, waiting for transfers between devices, body(): full_features = lax.all_gather(dispatched, 'exp', axis=1, tiled=True)  43.8 us
    reduce_scatter x1, waiting for transfers between devices, body(): lax.psum_scatter(terms.astype(jnp.bfloat16), 'exp', scatter_dimension=1,...  43.8 us
    dot_general x1, matrix products, local_scan(): jnp.einsum('hbij,bjhp->bihp', mixing, x_blocks, precision=highest)  18 us
    unnamed x1, blocking collectives  15.6 us
    reshape x2, local copies, waits for them, and re-layouts, body(): (local_out + handed).reshape(length, head_count, P_SIZE)  14.8 us
    reshape x2, local copies, waits for them, and re-layouts, body(): gate_input.astype(jnp.float32).reshape(length, head_count, P_SIZE)  14 us
  transfers between devices with their start and end apart: 5, of which 4 were waited for; matrix products, arithmetic and copies ran while one was open for 14% of the time, Pallas kernels for 0%

commit v1 on v0

--- a/solution.py
+++ b/solution.py
@@ -101,7 +101,10 @@
     places = jnp.arange(CAP, dtype=jnp.int32)[:, None] == expert_slot[None, :]
     picker = places.astype(jnp.bfloat16)
     dispatched = jnp.dot(picker, normed, preferred_element_type=jnp.float32).astype(jnp.bfloat16)
-    full_features = lax.all_gather(dispatched, "exp", axis=1, tiled=True)
+    n_dev = lax.axis_size("exp")
+    pieces = jnp.stack([dispatched for _ in range(n_dev)])
+    pieces = lax.all_to_all(pieces, "exp", split_axis=0, concat_axis=0)
+    full_features = jnp.concatenate(pieces, axis=1)
     up_act = jnp.dot(
         full_features,
         lax.all_gather(up_weight, "ctx", axis=0, tiled=True),

time: 377 us -> 289 us (0.77)
  waiting for transfers between devices: 183 us -> 43.5 us
  blocking collectives: 15.6 us -> 67.4 us
    all_to_all x0 -> x1, blocking collectives: none -> 52 us  [body(): pieces = lax.all_to_all(pieces, 'exp', split_axis=0, concat_axis=0)]
    all_gather x1, waiting for transfers between devices: 47.3 us -> 0.01 us  [body(): lax.all_gather(down_weight, 'ctx', axis=1, tiled=True)]
    all_gather x1, waiting for transfers between devices: 47.2 us -> 0.01 us  [body(): lax.all_gather(up_weight, 'ctx', axis=0, tiled=True)]
    all_gather x1 -> x0, waiting for transfers between devices: 43.8 us -> none  [body(): full_features = lax.all_gather(dispatched, 'exp', axis=1, tiled=True)]
  transfers between devices with their start and end apart: 5 -> 4, of which waited for: 4 -> 1; matrix products, arithmetic and copies ran while one was open for 14% -> 33% of each run, Pallas kernels for 0% -> 0%
where the time goes in v1:
time: 289 us; the launch traced here: 288 us
  local copies, waits for them, and re-layouts  74.7 us (26%)
  blocking collectives  67.4 us (23%)
  matrix products  62.1 us (21%)
  waiting for transfers between devices  43.5 us (15%)
  other arithmetic  25.6 us (9%)
  between operations  14 us (5%)
    all_to_all x1, blocking collectives, body(): pieces = lax.all_to_all(pieces, 'exp', split_axis=0, concat_axis=0)  52 us
    reduce_scatter x1, waiting for transfers between devices, body(): lax.psum_scatter(terms.astype(jnp.bfloat16), 'exp', scatter_dimension=1,...  42.1 us
    dot_general x1, matrix products, local_scan(): jnp.einsum('hbij,bjhp->bihp', mixing, x_blocks, precision=highest)  18 us
    unnamed x1, blocking collectives  15.5 us
    reshape x2, local copies, waits for them, and re-layouts, body(): (local_out + handed).reshape(length, head_count, P_SIZE)  14.9 us
    reshape x2, local copies, waits for them, and re-layouts, body(): mixer_input.astype(jnp.float32).reshape(blocks, BLK, head_count, P_SIZE)  14 us
    dot_general x1, matrix products, local_scan(): jnp.einsum('bin,hbi,bhnp->bihp', c_blocks, jnp.exp(cumulative), entering,...  12.5 us
    reshape x2, local copies, waits for them, and re-layouts, body(): gate_input.astype(jnp.float32).reshape(length, head_count, P_SIZE)  11.7 us
  transfers between devices with their start and end apart: 4, of which 1 were waited for; matrix products, arithmetic and copies ran while one was open for 33% of the time, Pallas kernels for 0%

profile of v1, /device:TPU:0, one launch (start us, length us, event | category | flops | bytes accessed | tf_op | source)
XLA Modules:
  0.0 287.8 jit_solution(13571739520266292853)
XLA Ops:
  6.5 0.9 copy.120
  7.4 4.5 %reduce_window_sum.33 = f32[16,8,128]{2,1,0:T(8,128)S(1)} reduce-window(f32[16,8,128]{2,1,0:T(8,128)S(1)} %bitcast.111, f32[]{:T(128)} %constant.28.clone.1), window={size=1x1x128 pad=0_0x0_0x127_0}, to_apply=%region_0.0 | reduce-window | flops 2080768 | bytes 131076 | tf_op jit(solution)/shard_map/jit(cumsum)/reduce_window_sum | solution.py:19
  12.4 0.3 slice_reduce_fusion
  12.9 0.9 copy.121
  13.7 0.6 exponential_bitcast_fusion.1
  14.4 0.7 multiply_exponential_fusion
  15.1 6.8 %reshape.101 = f32[8,128,16,64]{3,2,1,0:T(8,128)} reshape(bf16[1024,1024]{1,0:T(8,128)(2,1)} %param.15) | data formatting | bytes 6291456 | tf_op jit(solution)/shard_map/reshape | solution.py:66
  21.9 7.2 %copy.76 = f32[8,128,16,64]{1,3,2,0:T(8,128)} copy(f32[8,128,16,64]{3,2,1,0:T(8,128)} %reshape.101) | data formatting | bytes 8388608 | tf_op jit(solution)/shard_map/reshape | solution.py:66
  29.1 6.4 %fusion.20 = f32[8,16,128,64]{2,3,1,0:T(8,128)} fusion(bf16[8,128,128,1]{2,1,3,0:T(8,128)(2,1)S(1)} %bitcast.106, f32[8,128,16,64]{1,3,2,0:T(8,128)} %copy.76, f32[8,128,16]{1,2,0:T(8,128)S(1)} %copy.83, f32[8,16]{1,0:T(8,128)S(1)} %multiply_exponential_fusion), kind=kOutput, calls=%fused_computation.31 | convolution fusion | flops 1612709888 | bytes 8716800 | tf_op jit(solution)/shard_map/hbj,bjn,bjhp->bhnp/dot_general | solution.py:26
  35.5 21.8 %while.13 = (s32[]{:T(128)}, f32[16,128,64]{2,1,0:T(8,128)S(1)}, f32[8,16,128,64]{3,2,1,0:T(8,128)}, f32[8,16]{1,0:T(8,128)S(1)}, f32[8,16,128,64]{2,3,1,0:T(8,128)}, /*index=5*/s32[]{:T(128)}, s32[]{:T(128)}) while((s32[]{:T(128)}, f32[16,128,64]{2,1,0:T(8,128)S(1)}, f32[8,16,128,64]{3,2,1,0:T(8,128)}, f32[8,16]{1,0:T(8,128)S(1)}, ...), condition=%wide.region_2.3_spmd.clone, body=%wide.region_1.2_spmd.clone.sunk | while | flops 524291 | bytes 5243680 | solution.py:35
  35.5 1.0 bitcast_dynamic-update-slice_fusion.2
  36.6 1.1 constant_dynamic-slice_fusion.3
  37.6 0.3 copy.128
  38.2 1.1 bitcast_dynamic-update-slice_fusion.2
  39.3 1.1 constant_dynamic-slice_fusion.3
  40.4 0.3 copy.128
  41.0 1.1 bitcast_dynamic-update-slice_fusion.2
  42.1 1.1 constant_dynamic-slice_fusion.3
  43.1 0.3 copy.128
  43.7 1.1 bitcast_dynamic-update-slice_fusion.2
  44.8 1.1 constant_dynamic-slice_fusion.3
  45.9 0.3 copy.128
  46.2 0.2 bitcast_add_fusion.2
  46.4 1.1 bitcast_dynamic-update-slice_fusion.2
  47.5 1.1 constant_dynamic-slice_fusion.3
  48.6 0.3 copy.128
  49.2 1.1 bitcast_dynamic-update-slice_fusion.2
  50.2 1.1 constant_dynamic-slice_fusion.3
  51.3 0.3 copy.128
  51.9 1.1 bitcast_dynamic-update-slice_fusion.2
  53.0 1.1 constant_dynamic-slice_fusion.3
  54.0 0.3 copy.128
  54.4 0.2 bitcast_add_fusion.2
  54.6 1.1 bitcast_dynamic-update-slice_fusion.2
  55.7 1.1 constant_dynamic-slice_fusion.3
  56.8 0.3 copy.128
  57.4 0.9 copy.89
  58.3 0.7 all-gather.6.cloned.1.call-update
  59.1 0.7 all-gather.8.cloned.1.call-update
  59.9 0.6 dynamic-slice
  61.2 0.2 dynamic-update-slice
  61.4 15.5 %all-reduce = f32[128]{0:T(128)S(1)} all-reduce(f32[128]{0:T(128)S(1)} %dynamic-update-slice), channel_id=2, replica_groups=mesh['ctx'=8,'exp'=4] {'ctx'}, use_global_device_ids=true, to_apply=%add | all-reduce | flops 128 | bytes 1024
  77.0 0.9 copy.80
  77.9 4.5 %reshape.103 = f32[8,128,16,64]{3,2,1,0:T(8,128)} reshape(bf16[1024,1024]{1,0:T(8,128)(2,1)S(1)} %copy-done.3) | data formatting | bytes 6291456 | tf_op jit(solution)/shard_map/reshape | solution.py:93
  82.4 7.2 %copy.96 = f32[8,128,16,64]{1,3,2,0:T(8,128)} copy(f32[8,128,16,64]{3,2,1,0:T(8,128)} %reshape.103) | data formatting | bytes 8388608 | tf_op jit(solution)/shard_map/reshape | solution.py:93
  89.7 2.5 mul.135
  92.2 5.4 %copy.92 = f32[1024,1024]{1,0:T(8,128)} copy(f32[1024,1024]{0,1:T(8,128)} %bitcast.102) | data formatting | bytes 8388608 | tf_op jit(solution)/shard_map/mul | solution.py:66
  97.9 0.3 fusion.34
  98.2 12.5 %fusion.35 = f32[8,16,64,128]{3,2,1,0:T(8,128)} fusion(f32[8,16,128,64]{3,2,1,0:T(8,128)} %get-tuple-element.33, bf16[8,128,128,1]{2,1,3,0:T(8,128)(2,1)S(1)} %bitcast.99), kind=kOutput, calls=%fused_computation.60 | convolution fusion | flops 1610612736 | bytes 8650752 | tf_op jit(solution)/shard_map/bin,hbi,bhnp->bihp/dot_general | solution.py:38
  110.6 18.0 %fusion.2 = f32[8,16,64,128]{3,2,1,0:T(8,128)} fusion(f32[16,8,128]{2,0,1:T(8,128)S(1)} %copy_bitcast_fusion.2, f32[8,128,128]{2,1,0:T(8,128)S(1)} %fusion.34, f32[16,8,128]{2,0,1:T(8,128)S(1)} %copy.77, pred[128,128]{1,0:T(8,128)(4,1)S(1)} %iota_compare_fusion.3, f32[8,128,16,64]{1,3,2,0:T(8,128)S(1)} %copy-done.2, f32[8,16]{1,0:T(8,128)S(1)} %multiply_exponential_fusion), kind=kOutput, calls=%fused_computation.6 | convolution fusion | flops 1620049920 | bytes 9060864 | tf_op jit(solution)/shard_map/hbij,bjhp->bihp/dot_general | solution.py:24
  128.6 2.1 multiply_reduce_fusion
  130.8 9.6 %multiply_reduce_fusion.1 = (f32[8,128,16]{1,2,0:T(8,128)S(1)}, f32[8,128,16,64]{1,3,2,0:T(8,128)}) fusion(f32[8,128,16,64]{1,3,2,0:T(8,128)} %copy.96, f32[8,128,16,64]{1,3,2,0:T(8,128)} %copy.76, f32[16]{0:T(128)S(1)} %copy-done.10, f32[8,16]{1,0:T(8,128)S(1)} %multiply_exponential_fusion, bf16[8,128,128,1]{2,1,3,0:T(8,128)(2,1)S(1)} %bitcast.100, ...), kind=kOutput, calls=%fused_computation.20 | convolution fusion | flops 1625276416 | bytes 21955136 | tf_op jit(solution)/shard_map/bin,hbi,hnp->bihp/dot_general | solution.py:88
  140.3 7.2 %copy.113 = f32[8,128,16,64]{3,2,1,0:T(8,128)} copy(f32[8,128,16,64]{1,3,2,0:T(8,128)} %get-tuple-element.89) | data formatting | bytes 8388608 | tf_op jit(solution)/shard_map/reshape | solution.py:89
  147.5 7.7 %reshape.102 = f32[1024,1024]{1,0:T(8,128)} reshape(f32[8,128,16,64]{3,2,1,0:T(8,128)} %copy.113) | data formatting | bytes 8388608 | tf_op jit(solution)/shard_map/reshape | solution.py:89
  155.2 2.5 mul.146
  157.7 5.4 %copy.98 = f32[1024,1024]{1,0:T(8,128)} copy(f32[1024,1024]{0,1:T(8,128)} %bitcast.103) | data formatting | bytes 8388608 | tf_op jit(solution)/shard_map/mul | solution.py:97
  163.1 7.0 %multiply_convert_fusion = bf16[1024,1024]{1,0:T(8,128)(2,1)S(1)} fusion(f32[1024,1024]{1,0:T(8,128)} %copy.98, f32[1024,1024]{1,0:T(8,128)} %reshape.102, f32[1024,1024]{1,0:T(8,128)} %copy.92, f32[1024]{0:T(1024)S(1)} %copy-done.9, f32[1024]{0:T(1024)S(1)} %mul.131, bf16[1024,1024]{1,0:T(8,128)(2,1)S(1)} %copy-done.3, bf16[1024,1024]{1,0:T(8,128)(2,1)} %param.15), kind=kLoop, calls=%fused_computation.19 | loop fusion | flops 13631488 | bytes 18882560 | tf_op jit(solution)/shard_map/convert_element_type | solution.py:99
  170.1 1.3 copy-done.4
  171.4 0.7 convolution_convert_fusion.1
  172.2 0.2 copy.99
  172.5 52.0 %all_to_all.5 = bf16[4,256,1024]{1,2,0:T(8,128)(2,1)} all-to-all(bf16[4,256,1024]{1,2,0:T(8,128)(2,1)S(1)} %stack.2), channel_id=1, replica_groups=mesh['ctx'=8,'exp'=4] {'exp'}, dimensions={0} | all-to-all | bytes 4194304 | tf_op jit(solution)/shard_map/all_to_all | solution.py:106
  224.5 11.4 %convolution_convert_fusion = bf16[256,4096]{1,0:T(8,128)(2,1)} fusion(bf16[768,4096]{1,0:T(8,128)(2,1)} %all-gather.8.cloned.1.call-done, bf16[256,4096]{0,1:T(8,128)(2,1)} %bitcast.105, bf16[4096,768]{1,0:T(8,128)(2,1)} %all-gather.6.cloned.1.call-done), kind=kOutput, calls=%fused_computation.12 | convolution fusion | flops 3223257088 | bytes 16777216 | tf_op jit(solution)/shard_map/dot_general | solution.py:114
  235.9 42.1 %reduce-scatter.2.cloned.1.call-done = bf16[256,1024]{1,0:T(8,128)(2,1)} async-done(((bf16[256,4096]{1,0:T(8,128)(2,1)}), bf16[256,1024]{1,0:T(8,128)(2,1)}) %reduce-scatter.2.cloned.1.call-update) | async-done | bytes 524304 | tf_op jit(solution)/shard_map/reduce_scatter | solution.py:119
  278.0 3.3 %add_convert_fusion = bf16[1024,1024]{1,0:T(8,128)(2,1)} fusion(bf16[1024,1024]{1,0:T(8,128)(2,1)S(1)} %copy-done.5, bf16[256,1024]{1,0:T(8,128)(2,1)} %reduce-scatter.2.cloned.1.call-done, f32[1024]{0:T(1024)S(1)} %copy-done.12, s32[1024]{0:T(1024)S(1)} %copy-done.11), kind=kOutput, calls=%fused_computation.18 | convolution fusion | flops 541327360 | bytes 4726784 | tf_op jit(solution)/shard_map/dot_general | solution.py:123
  (76 shorter events, 2.8 us)
Async XLA Ops:
  6.5 91.3 %copy-start = (bf16[1024,128]{1,0:T(8,128)(2,1)S(1)}, bf16[1024,128]{1,0:T(8,128)(2,1)}, u32[]{:S(2)}) copy-start(bf16[1024,128]{1,0:T(8,128)(2,1)} %param.20) | copy-start | bytes 786436
  6.5 122.1 %all-gather.10.cloned.1.call-start = ((), (), s32[]{:S(2)}) async-start(), calls=%async_computation.5 | async-start | bytes 2359296 | tf_op jit(solution)/shard_map/all_gather | solution.py:78
  21.9 7.2 %copy-start.6 = (bf16[1024,128]{1,0:T(8,128)(2,1)S(1)}, bf16[1024,128]{1,0:T(8,128)(2,1)}, u32[]{:S(2)}) copy-start(bf16[1024,128]{1,0:T(8,128)(2,1)} %param.19) | copy-start | bytes 786436
  35.5 24.4 %copy-start.13 = (u32[32]{0:T(128)S(1)}, u32[32]{0:T(128)}, u32[]{:S(2)}) copy-start(u32[32]{0:T(128)} %constant.54) | copy-start | bytes 388
  57.4 20.5 %copy-start.3 = (bf16[1024,1024]{1,0:T(8,128)(2,1)S(1)}, bf16[1024,1024]{1,0:T(8,128)(2,1)}, u32[]{:S(2)}) copy-start(bf16[1024,1024]{1,0:T(8,128)(2,1)} %param.22) | copy-start | bytes 6291460
  58.3 166.2 %all-gather.6.cloned.1.call-start = ((), (), s32[]{:S(2)}) async-start(), calls=%async_computation.2 | async-start | bytes 7077888 | tf_op jit(solution)/shard_map/all_gather | solution.py:110
  59.0 165.5 %all-gather.8.cloned.1.call-start = ((), (), s32[]{:S(2)}) async-start(), calls=%async_computation.3 | async-start | bytes 7077888 | tf_op jit(solution)/shard_map/all_gather | solution.py:116
  59.8 218.2 %reduce-scatter.2.cloned.1.call-start = ((), (), s32[]{:S(2)}) async-start(), calls=%async_computation.4 | async-start | bytes 2621440 | tf_op jit(solution)/shard_map/reduce_scatter | solution.py:119
  92.2 5.4 %copy-start.10 = (f32[16]{0:T(128)S(1)}, f32[16]{0:T(128)}, u32[]{:S(2)}) copy-start(f32[16]{0:T(128)} %param.21) | copy-start | bytes 196
  92.2 5.7 %copy-start.8 = (f32[16,1024]{1,0:T(8,128)S(1)}, f32[16,1024]{1,0:T(8,128)}, u32[]{:S(2)}) copy-start(f32[16,1024]{1,0:T(8,128)} %param.17) | copy-start | bytes 196612
  92.2 5.7 %copy-start.7 = (bf16[1024,128]{1,0:T(8,128)(2,1)S(1)}, bf16[1024,128]{1,0:T(8,128)(2,1)}, u32[]{:S(2)}) copy-start(bf16[1024,128]{1,0:T(8,128)(2,1)} %param.19) | copy-start | bytes 786436
  98.2 12.5 %copy-start.2 = (f32[8,128,16,64]{1,3,2,0:T(8,128)S(1)}, f32[8,128,16,64]{1,3,2,0:T(8,128)}, u32[]{:S(2)}) copy-start(f32[8,128,16,64]{1,3,2,0:T(8,128)} %copy.76) | copy-start | bytes 12582916
  157.7 5.4 %copy-start.9 = (f32[1024]{0:T(1024)S(1)}, f32[1024]{0:T(1024)}, u32[]{:S(2)}) copy-start(f32[1024]{0:T(1024)} %param.23) | copy-start | bytes 12292
  163.1 8.3 %copy-start.11 = (s32[1024]{0:T(1024)S(1)}, s32[1024]{0:T(1024)}, u32[]{:S(2)}) copy-start(s32[1024]{0:T(1024)} %param.26) | copy-start | bytes 12292
  170.1 1.3 copy-start.4
  224.5 53.5 %copy-start.5 = (bf16[1024,1024]{1,0:T(8,128)(2,1)S(1)}, bf16[1024,1024]{1,0:T(8,128)(2,1)}, u32[]{:S(2)}) copy-start(bf16[1024,1024]{1,0:T(8,128)(2,1)} %copy-done.4) | copy-start | bytes 6291460
  224.5 53.5 %copy-start.12 = (f32[1024]{0:T(1024)S(1)}, f32[1024]{0:T(1024)}, u32[]{:S(2)}) copy-start(f32[1024]{0:T(1024)} %param.27) | copy-start | bytes 12292
  224.5 56.7 %copy-start.1 = (bf16[1024,128]{1,0:T(8,128)(2,1)S(1)}, bf16[1024,128]{1,0:T(8,128)(2,1)}, u32[]{:S(2)}) copy-start(bf16[1024,128]{1,0:T(8,128)(2,1)} %param.20) | copy-start | bytes 786436
Sparse Core Ops, SparseCore 0:
  58.4 30.5 all-gather.9
  90.9 45.3 all-gather.5
  138.2 46.5 all-gather.7
  236.0 41.9 reduce-scatter.1
